TPU v7x, 32 devices: a whole 2x2x4 slice. The times are simulated.
32 devices in a mesh: ctx: 8 (over z, x), dp: 4 (over y, core).
Axes of the slice: x: 2, y: 2, z: 4, core: 2. Of those that a mesh axis runs over, the one named last changes fastest.
Arguments:
- queries: bfloat16 [4, 2048, 1024], P('dp', 'ctx'), may hold values from -8 to 8
- keys: bfloat16 [4, 2048, 1024], P('dp', 'ctx'), may hold values from -8 to 8
- values: bfloat16 [4, 2048, 1024], P('dp', 'ctx'), may hold values from -6 to 6
- cotangent: bfloat16 [4, 2048, 2048], P('dp', 'ctx'), may hold values from -6 to 6
- proj_weight: bfloat16 [1024, 2048], P('dp'), may hold values from -0.1875 to 0.1875
- pattern: int32 [4, 8, 16, 2], P('dp'), may hold values 0 or 1
Outputs:
- projected: bfloat16 [4, 2048, 2048], P('dp', 'ctx')
- grad_query: bfloat16 [4, 2048, 1024], P('dp', 'ctx')
- grad_key: bfloat16 [4, 2048, 1024], P('dp', 'ctx')
- grad_value: bfloat16 [4, 2048, 1024], P('dp', 'ctx')
- grad_proj: float32 [1024, 2048], P('dp', 'ctx')
Inputs may be any that keep to these rules, and one draw needn't show every extreme that they name: `pattern`: entries with o = 0 or with q - o < 1 are not read.
All inputs are finite; a program needn't handle non-finite values. No bound on the sum of `pattern` on one device may be relied on, other than what follows from the above.
Results may differ from a plain program's by a relative error of at most 0.0085.
The roundings to bfloat16 on the way count: a program that leaves them out, or rounds other values in their place, can miss the bound.
Values may be sent and summed in bfloat16 or wider, within the bound.
No kernel may reach another device: no remote copies, remote signals or barrier semaphores. Data moves between devices by JAX's collectives and lax.ppermute only.
A program may use at most 128 MiB of HBM per device.

v0:
```python
import jax
import jax.numpy as jnp
from jax import lax
from jax.sharding import PartitionSpec as P

HEADS = 8
HDIM = 128
BLK = 128
BLK_DEV = 2
WIN = 2
masked_value = -1e30


def shifted(value, axis, steps):
    count = lax.axis_size(axis)
    leading, last = (max(0, -steps), min(count, count - steps))
    return lax.ppermute(value, axis, [(source, source + steps) for source in range(leading, last)])


def spread(block, axis, holder):
    block = jnp.where(lax.axis_index(axis) == holder, block, jnp.zeros_like(block))
    return lax.psum(block, axis)


def product(form, left, right):
    return jnp.einsum(form, left, right, preferred_element_type=jnp.float32)


def block_masks(pattern_rows, query_blocks):
    column = jnp.arange(WIN * BLK, dtype=jnp.int32)
    within = jnp.arange(BLK, dtype=jnp.int32)
    offsets = WIN - 1 - jnp.arange(WIN, dtype=jnp.int32)
    flipped = jnp.flip(pattern_rows, axis=2) == 1
    key_blocks = query_blocks[:, None] - offsets[None, :]
    permitted = (flipped | (offsets == 0)[None, None, :]) & (key_blocks >= 1)[:, None, :]
    expanded = jnp.repeat(permitted, BLK, axis=2)
    causal = (column[None, :] < (WIN - 1) * BLK) | (
        column[None, :] - (WIN - 1) * BLK <= within[:, None]
    )
    key_mask = expanded[:, :, None, :] & causal[None, None, :, :]
    sink_mask = (query_blocks[:, None, None] > 0) | (within[None, None, :] <= within[None, :, None])
    return (key_mask, sink_mask[:, None, :, :])


def attend_scores(queries_b, key_window, sink_keys, key_mask, sink_mask):
    inverse_root = HDIM ** (-0.5)
    scores = product("nqhd,nkhd->nhqk", queries_b, key_window) * inverse_root
    sink_scores = product("nqhd,khd->nhqk", queries_b, sink_keys) * inverse_root
    return (
        jnp.where(key_mask, scores, masked_value),
        jnp.where(sink_mask, sink_scores, masked_value),
    )


def forward_blocks(
    queries_b, key_window, value_window, sink_keys, sink_values, key_mask, sink_mask
):
    scores, sink_scores = attend_scores(queries_b, key_window, sink_keys, key_mask, sink_mask)
    row_max = jnp.maximum(jnp.max(scores, axis=-1), jnp.max(sink_scores, axis=-1))
    row_total = jnp.sum(jnp.exp(scores - row_max[..., None]), axis=-1) + jnp.sum(
        jnp.exp(sink_scores - row_max[..., None]), axis=-1
    )
    log_total = row_max + jnp.log(row_total)
    weights = jnp.exp(scores - log_total[..., None]).astype(jnp.bfloat16)
    sink_weights = jnp.exp(sink_scores - log_total[..., None]).astype(jnp.bfloat16)
    attended = product("nhqk,nkhd->nqhd", weights, value_window) + product(
        "nhqk,khd->nqhd", sink_weights, sink_values
    )
    return (attended.astype(jnp.bfloat16), log_total)


def backward_blocks(
    queries_b,
    key_window,
    value_window,
    sink_keys,
    sink_values,
    key_mask,
    sink_mask,
    log_total,
    out_grad,
    row_delta,
):
    inverse_root = HDIM ** (-0.5)
    scores, sink_scores = attend_scores(queries_b, key_window, sink_keys, key_mask, sink_mask)
    weights = jnp.exp(scores - log_total[..., None])
    sink_weights = jnp.exp(sink_scores - log_total[..., None])
    prob_grad = product("nqhd,nkhd->nhqk", out_grad, value_window)
    sink_prob_grad = product("nqhd,khd->nhqk", out_grad, sink_values)
    score_grad = (weights * (prob_grad - row_delta[..., None])).astype(jnp.bfloat16)
    sink_score_grad = (sink_weights * (sink_prob_grad - row_delta[..., None])).astype(jnp.bfloat16)
    query_grad = inverse_root * (
        product("nhqk,nkhd->nqhd", score_grad, key_window)
        + product("nhqk,khd->nqhd", sink_score_grad, sink_keys)
    )
    window_key_grad = inverse_root * product("nhqk,nqhd->nkhd", score_grad, queries_b)
    window_value_grad = product("nhqk,nqhd->nkhd", weights.astype(jnp.bfloat16), out_grad)
    sink_key_grad = inverse_root * product("nhqk,nqhd->khd", sink_score_grad, queries_b)
    sink_value_grad = product("nhqk,nqhd->khd", sink_weights.astype(jnp.bfloat16), out_grad)
    return (query_grad, window_key_grad, window_value_grad, sink_key_grad, sink_value_grad)


def make_windows(extended, first):
    pieces = [
        extended[(number + first) * BLK : (number + first + WIN) * BLK] for number in range(BLK_DEV)
    ]
    return jnp.stack(pieces).reshape(BLK_DEV, WIN * BLK, HEADS, HDIM)


def place_windows(window_grad):
    flat = window_grad.reshape(BLK_DEV, WIN * BLK, HEADS * HDIM)
    placed = jnp.zeros((2 * BLK_DEV * BLK, HEADS * HDIM), jnp.float32)
    for number in range(BLK_DEV):
        placed = placed + jnp.pad(
            flat[number], (((number + 1) * BLK, (2 * BLK_DEV - number - 1 - WIN) * BLK), (0, 0))
        )
    return placed


def body(queries, keys, values, cotangent, proj_weight, pattern):
    query_rows = queries[0]
    key_rows = keys[0]
    value_rows = values[0]
    grad_output = cotangent[0]
    pattern_doc = pattern[0]
    rows = query_rows.shape[0]
    width_heads = query_rows.shape[1]
    context_index = lax.axis_index("ctx")
    context_count = lax.axis_size("ctx")
    document_count = lax.axis_size("dp")
    prev_keys, prev_values = shifted((key_rows, value_rows), "ctx", 1)
    first_keys, first_values = (
        spread(key_rows[:BLK], "ctx", 0),
        spread(value_rows[:BLK], "ctx", 0),
    )
    full_weight = lax.all_gather(proj_weight, "dp", axis=0, tiled=True)
    query_blocks = context_index * BLK_DEV + jnp.arange(BLK_DEV, dtype=jnp.int32)
    pattern_rows = jnp.transpose(
        lax.dynamic_slice_in_dim(pattern_doc, context_index * BLK_DEV, BLK_DEV, 1), (1, 0, 2)
    )
    key_mask, sink_mask = block_masks(pattern_rows, query_blocks)
    key_window = make_windows(jnp.concatenate([prev_keys, key_rows], axis=0), 1)
    value_window = make_windows(jnp.concatenate([prev_values, value_rows], axis=0), 1)
    query_blocked = query_rows.reshape(BLK_DEV, BLK, HEADS, HDIM)
    sink_keys = first_keys.reshape(BLK, HEADS, HDIM)
    sink_values = first_values.reshape(BLK, HEADS, HDIM)
    attended, log_total = forward_blocks(
        query_blocked, key_window, value_window, sink_keys, sink_values, key_mask, sink_mask
    )
    attended_rows = attended.reshape(rows, width_heads)
    projected = jnp.dot(attended_rows, full_weight, preferred_element_type=jnp.float32).astype(
        jnp.bfloat16
    )
    grad_attended = lax.dot_general(
        grad_output, full_weight, (((1,), (1,)), ((), ())), preferred_element_type=jnp.float32
    ).astype(jnp.bfloat16)
    weight_scale = float(rows * context_count * document_count) ** (-0.5)
    partial_sum = lax.psum_scatter(
        lax.dot_general(
            attended_rows, grad_output, (((0,), (0,)), ((), ())), preferred_element_type=jnp.float32
        )
        * weight_scale,
        "dp",
        scatter_dimension=0,
        tiled=True,
    )
    grad_proj = lax.psum_scatter(partial_sum, "ctx", scatter_dimension=1, tiled=True)
    row_delta = jnp.sum(
        grad_attended.astype(jnp.float32).reshape(rows, HEADS, HDIM)
        * attended_rows.astype(jnp.float32).reshape(rows, HEADS, HDIM),
        axis=-1,
    )
    delta_blocked = jnp.transpose(row_delta.reshape(BLK_DEV, BLK, HEADS), (0, 2, 1))
    grad_blocked = grad_attended.reshape(BLK_DEV, BLK, HEADS, HDIM)
    query_grad, window_key, window_value, sink_key, sink_value = backward_blocks(
        query_blocked,
        key_window,
        value_window,
        sink_keys,
        sink_values,
        key_mask,
        sink_mask,
        log_total,
        grad_blocked,
        delta_blocked,
    )
    sink_key_sum, sink_value_sum = lax.psum((sink_key, sink_value), "ctx")
    placed_keys = place_windows(window_key)
    placed_values = place_windows(window_value)
    later_keys, later_values = shifted((placed_keys[:rows], placed_values[:rows]), "ctx", -1)
    own_key = placed_keys[rows:] + later_keys
    own_value = placed_values[rows:] + later_values
    leading = (context_index == 0).astype(jnp.float32)
    own_key = jnp.concatenate(
        [own_key[:BLK] + leading * sink_key_sum.reshape(BLK, width_heads), own_key[BLK:]], axis=0
    )
    own_value = jnp.concatenate(
        [own_value[:BLK] + leading * sink_value_sum.reshape(BLK, width_heads), own_value[BLK:]],
        axis=0,
    )
    return (
        projected[None],
        query_grad.reshape(rows, width_heads).astype(jnp.bfloat16)[None],
        own_key.astype(jnp.bfloat16)[None],
        own_value.astype(jnp.bfloat16)[None],
        grad_proj,
    )


def solution(mesh):
    return jax.shard_map(
        body,
        mesh=mesh,
        in_specs=(
            P("dp", "ctx", None),
            P("dp", "ctx", None),
            P("dp", "ctx", None),
            P("dp", "ctx", None),
            P("dp", None),
            P("dp", None, None, None),
        ),
        out_specs=(
            P("dp", "ctx", None),
            P("dp", "ctx", None),
            P("dp", "ctx", None),
            P("dp", "ctx", None),
            P("dp", "ctx"),
        ),
        check_vma=False,
    )
```

profile of v0, /device:TPU:0, one launch (start us, length us, event | category | flops | bytes accessed | tf_op | source)
XLA Modules:
  0.0 304.7 jit_solution(7784377283178281256)
XLA Ops:
  13.1 5.7 %collective-permute-start = (bf16[256,1024]{0,1:T(8,128)(2,1)S(1)}, bf16[256,1024]{0,1:T(8,128)(2,1)}, u32[]{:S(2)}, u32[]{:S(2)}) collective-permute-start(bf16[256,1024]{0,1:T(8,128)(2,1)S(1)} %bitcast.149), channel_id=1, source_target_pairs={{0,4},{4,8},{8,12},{12,16},{16,20},{20,24},{24,28},{1,5},{5,9},{9,... | collective-permute-start | bytes 1572872 | tf_op jit(solution)/shard_map/ppermute | solution.py:17
  18.8 3.4 %collective-permute-start.1 = (bf16[256,1024]{0,1:T(8,128)(2,1)S(1)}, bf16[256,1024]{0,1:T(8,128)(2,1)}, u32[]{:S(2)}, u32[]{:S(2)}) collective-permute-start(bf16[256,1024]{0,1:T(8,128)(2,1)S(1)} %bitcast.146), channel_id=1, source_target_pairs={{0,4},{4,8},{8,12},{12,16},{16,20},{20,24},{24,28},{1,5},{5,9},{9,... | collective-permute-start | bytes 1572872 | tf_op jit(solution)/shard_map/ppermute | solution.py:17
  26.2 5.9 %collective-permute-done = bf16[256,1024]{0,1:T(8,128)(2,1)} collective-permute-done((bf16[256,1024]{0,1:T(8,128)(2,1)S(1)}, bf16[256,1024]{0,1:T(8,128)(2,1)}, u32[]{:S(2)}, u32[]{:S(2)}) %collective-permute-start) | collective-permute-done | bytes 524320 | tf_op jit(solution)/shard_map/ppermute | solution.py:17
  34.1 9.0 %collective-permute-done.1 = bf16[256,1024]{0,1:T(8,128)(2,1)} collective-permute-done((bf16[256,1024]{0,1:T(8,128)(2,1)S(1)}, bf16[256,1024]{0,1:T(8,128)(2,1)}, u32[]{:S(2)}, u32[]{:S(2)}) %collective-permute-start.1) | collective-permute-done | bytes 524320 | tf_op jit(solution)/shard_map/ppermute | solution.py:17
  45.1 49.3 %all-reduce.11.cloned.1.call-done = (bf16[128,8,128]{2,0,1:T(8,128)(2,1)}, bf16[128,8,128]{2,0,1:T(8,128)(2,1)}) async-done(((bf16[128,8,128]{2,0,1:T(8,128)(2,1)}, bf16[128,8,128]{2,0,1:T(8,128)(2,1)}), (bf16[128,8,128]{2,0,1:T(8,128)(2,1)}, bf16[128,8,128]{2,0,1:T(8,128)(2,1)})) %all-reduce.11.cloned.1.call-update) | async-done | bytes 524304 | tf_op jit(solution)/shard_map/psum | solution.py:22
  95.7 2.4 fusion.48
  102.5 4.6 %convolution_multiply_fusion = f32[1024,2048]{1,0:T(8,128)} fusion(bf16[1,256,2048]{2,1,0:T(8,128)(2,1)S(1)} %copy-done, bf16[32,8,8,128]{3,2,1,0:T(8,128)(2,1)S(1)} %bitcast.156), kind=kOutput, calls=%fused_computation | convolution fusion | flops 1075838976 | bytes 9961472 | tf_op jit(solution)/shard_map/dot_general | solution.py:159
  107.2 2.3 copy.155
  109.5 3.5 %convolution_convert_fusion.1 = bf16[256,1024]{1,0:T(8,128)(2,1)S(1)} fusion(bf16[1024,2048]{1,0:T(8,128)(2,1)} %all-gather.2.cloned.1.call-done, bf16[1,256,2048]{2,1,0:T(8,128)(2,1)S(1)} %copy-done), kind=kOutput, calls=%fused_computation.30 | convolution fusion | flops 1074003968 | bytes 5767168 | tf_op jit(solution)/shard_map/dot_general | solution.py:154
  116.4 2.2 copy.174
  119.5 2.8 convolution_bitcast_fusion.6
  124.8 2.1 copy.172
  132.1 2.1 copy.164
  134.2 2.1 convert_element_type.79
  136.3 41.4 %reduce-scatter.3.cloned.1.call-done = f32[256,2048]{1,0:T(8,128)} async-done(((f32[1024,2048]{1,0:T(8,128)}), f32[256,2048]{1,0:T(8,128)}) %reduce-scatter.3.cloned.1.call-update) | async-done | bytes 2097168 | tf_op jit(solution)/shard_map/reduce_scatter | solution.py:158
  181.0 2.5 copy.169
  183.5 2.5 copy.168
  186.0 2.3 pad_add_fusion.1
  193.5 2.2 fusion
  195.8 9.9 %all-reduce.9.cloned.1.call-done = (f32[128,8,128]{2,0,1:T(8,128)}, f32[128,8,128]{2,0,1:T(8,128)}) async-done(((f32[128,8,128]{2,0,1:T(8,128)}, f32[128,8,128]{2,0,1:T(8,128)}), (f32[128,8,128]{2,0,1:T(8,128)}, f32[128,8,128]{2,0,1:T(8,128)})) %all-reduce.9.cloned.1.call-update) | async-done | bytes 1048592 | tf_op jit(solution)/shard_map/psum | solution.py:187
  209.6 7.0 %collective-permute-done.2 = f32[256,1024]{0,1:T(8,128)} collective-permute-done((f32[256,1024]{0,1:T(8,128)}, f32[256,1024]{0,1:T(8,128)}, u32[]{:S(2)}, u32[]{:S(2)}) %collective-permute-start.2) | collective-permute-done | bytes 1048608 | tf_op jit(solution)/shard_map/ppermute | solution.py:17
  218.9 2.1 copy.178
  224.9 18.4 %collective-permute-done.3 = f32[256,1024]{0,1:T(8,128)} collective-permute-done((f32[256,1024]{0,1:T(8,128)}, f32[256,1024]{0,1:T(8,128)}, u32[]{:S(2)}, u32[]{:S(2)}) %collective-permute-start.3) | collective-permute-done | bytes 1048608 | tf_op jit(solution)/shard_map/ppermute | solution.py:17
  245.9 51.6 %reduce-scatter.5.cloned.1.call-done = f32[256,256]{1,0:T(8,128)} async-done(((f32[256,2048]{1,0:T(8,128)}), f32[256,256]{1,0:T(8,128)}) %reduce-scatter.5.cloned.1.call-update) | async-done | bytes 262160 | tf_op jit(solution)/shard_map/reduce_scatter | solution.py:167
  (144 shorter events, 51.7 us)
Async XLA Ops:
  8.0 94.5 %copy-start = (bf16[1,256,2048]{2,1,0:T(8,128)(2,1)S(1)}, bf16[1,256,2048]{2,1,0:T(8,128)(2,1)}, u32[]{:S(2)}) copy-start(bf16[1,256,2048]{2,1,0:T(8,128)(2,1)} %param.9) | copy-start | bytes 3145732
  8.0 86.4 %all-reduce.11.cloned.1.call-start = ((), (), s32[]{:S(2)}) async-start(), calls=%async_computation.6 | async-start | bytes 1048576 | tf_op jit(solution)/shard_map/psum | solution.py:22
  10.7 12.5 %copy-start.28 = (bf16[1,256,1024]{2,1,0:T(8,128)(2,1)S(1)}, bf16[1,256,1024]{2,1,0:T(8,128)(2,1)}, u32[]{:S(2)}) copy-start(bf16[1,256,1024]{2,1,0:T(8,128)(2,1)} %param.6) | copy-start | bytes 1572868
  12.5 97.0 %all-gather.2.cloned.1.call-start = ((), (), s32[]{:S(2)}) async-start(), calls=%async_computation.2 | async-start | bytes 5242880 | tf_op jit(solution)/shard_map/all_gather | solution.py:136
  13.0 164.7 %reduce-scatter.3.cloned.1.call-start = ((), (), s32[]{:S(2)}) async-start(), calls=%async_computation.3 | async-start | bytes 10485760 | tf_op jit(solution)/shard_map/reduce_scatter | solution.py:158
  13.1 19.0 %collective-permute-start = (bf16[256,1024]{0,1:T(8,128)(2,1)S(1)}, bf16[256,1024]{0,1:T(8,128)(2,1)}, u32[]{:S(2)}, u32[]{:S(2)}) collective-permute-start(bf16[256,1024]{0,1:T(8,128)(2,1)S(1)} %bitcast.149), channel_id=1, source_target_pairs={{0,4},{4,8},{8,12},{12,16},{16,20},{20,24},{24,28},{1,5},{5,9},{9,... | collective-permute-start | bytes 1572872 | tf_op jit(solution)/shard_map/ppermute | solution.py:17
  18.8 24.3 %collective-permute-start.1 = (bf16[256,1024]{0,1:T(8,128)(2,1)S(1)}, bf16[256,1024]{0,1:T(8,128)(2,1)}, u32[]{:S(2)}, u32[]{:S(2)}) collective-permute-start(bf16[256,1024]{0,1:T(8,128)(2,1)S(1)} %bitcast.146), channel_id=1, source_target_pairs={{0,4},{4,8},{8,12},{12,16},{16,20},{20,24},{24,28},{1,5},{5,9},{9,... | collective-permute-start | bytes 1572872 | tf_op jit(solution)/shard_map/ppermute | solution.py:17
  23.3 71.1 %copy-start.10 = (bf16[32,8,8,128]{3,2,1,0:T(8,128)(2,1)}, bf16[32,8,8,128]{3,2,1,0:T(8,128)(2,1)S(1)}, u32[]{:S(2)}) copy-start(bf16[32,8,8,128]{3,2,1,0:T(8,128)(2,1)S(1)} %copy.199) | copy-start | bytes 1572868
  95.7 4.2 %copy-start.1 = (f32[2,8,128,128]{2,3,0,1:T(8,128)}, f32[2,8,128,128]{2,3,0,1:T(8,128)S(1)}, u32[]{:S(2)}) copy-start(f32[2,8,128,128]{2,3,0,1:T(8,128)S(1)} %get-tuple-element.31) | copy-start | bytes 3145732
  107.1 98.5 %all-reduce.9.cloned.1.call-start = ((), (), s32[]{:S(2)}) async-start(), calls=%async_computation.5 | async-start | bytes 2097152 | tf_op jit(solution)/shard_map/psum | solution.py:187
  118.6 3.6 %copy-start.2 = (f32[2,8,128,128]{2,3,0,1:T(8,128)S(1)}, f32[2,8,128,128]{2,3,0,1:T(8,128)}, u32[]{:S(2)}) copy-start(f32[2,8,128,128]{2,3,0,1:T(8,128)} %copy-done.1) | copy-start | bytes 3145732
  118.6 3.6 %copy-start.18 = (bf16[2,128,8,128]{1,3,0,2:T(8,128)(2,1)S(1)}, bf16[2,128,8,128]{1,3,0,2:T(8,128)(2,1)}, u32[]{:S(2)}) copy-start(bf16[2,128,8,128]{1,3,0,2:T(8,128)(2,1)} %copy.174) | copy-start | bytes 1572868
  119.5 3.9 %copy-start.11 = (bf16[32,8,8,128]{3,2,1,0:T(8,128)(2,1)S(1)}, bf16[32,8,8,128]{3,2,1,0:T(8,128)(2,1)}, u32[]{:S(2)}) copy-start(bf16[32,8,8,128]{3,2,1,0:T(8,128)(2,1)} %copy-done.10) | copy-start | bytes 1572868
  123.4 3.5 %copy-start.29 = (f32[256,8]{0,1:T(8,128)S(1)}, f32[256,8]{0,1:T(8,128)}, u32[]{:S(2)}) copy-start(f32[256,8]{0,1:T(8,128)} %copy.156) | copy-start | bytes 24580
  124.5 173.0 %reduce-scatter.5.cloned.1.call-start = ((), (), s32[]{:S(2)}) async-start(), calls=%async_computation.4 | async-start | bytes 2359296 | tf_op jit(solution)/shard_map/reduce_scatter | solution.py:167
  186.0 3.6 %copy-start.12 = (bf16[2,128,8,128]{1,3,2,0:T(8,128)(2,1)S(1)}, bf16[2,128,8,128]{1,3,2,0:T(8,128)(2,1)}, u32[]{:S(2)}) copy-start(bf16[2,128,8,128]{1,3,2,0:T(8,128)(2,1)} %copy.172) | copy-start | bytes 1572868
  188.3 28.2 %collective-permute-start.2 = (f32[256,1024]{0,1:T(8,128)}, f32[256,1024]{0,1:T(8,128)}, u32[]{:S(2)}, u32[]{:S(2)}) collective-permute-start(f32[256,1024]{0,1:T(8,128)} %pad_add_fusion.1), channel_id=1, source_target_pairs={{4,0},{8,4},{12,8},{16,12},{20,16},{24,20},{28,24},{5,1},{9,5},{13... | collective-permute-start | bytes 3145736 | tf_op jit(solution)/shard_map/ppermute | solution.py:17
  191.3 52.0 %collective-permute-start.3 = (f32[256,1024]{0,1:T(8,128)}, f32[256,1024]{0,1:T(8,128)}, u32[]{:S(2)}, u32[]{:S(2)}) collective-permute-start(f32[256,1024]{0,1:T(8,128)} %pad_add_fusion), channel_id=1, source_target_pairs={{4,0},{8,4},{12,8},{16,12},{20,16},{24,20},{28,24},{5,1},{9,5},{13... | collective-permute-start | bytes 3145736 | tf_op jit(solution)/shard_map/ppermute | solution.py:17
  195.8 20.8 %copy-start.4 = (f32[1,256,8,128]{1,3,2,0:T(8,128)S(1)}, f32[1,256,8,128]{1,3,2,0:T(8,128)}, u32[]{:S(2)}) copy-start(f32[1,256,8,128]{1,3,2,0:T(8,128)} %copy.169) | copy-start | bytes 3145732
  195.8 20.8 %copy-start.5 = (f32[1,256,8,128]{1,3,2,0:T(8,128)S(1)}, f32[1,256,8,128]{1,3,2,0:T(8,128)}, u32[]{:S(2)}) copy-start(f32[1,256,8,128]{1,3,2,0:T(8,128)} %copy.168) | copy-start | bytes 3145732
  209.6 8.4 %copy-start.22 = (f32[128,8,128]{0,2,1:T(8,128)S(1)}, f32[128,8,128]{0,2,1:T(8,128)}, u32[]{:S(2)}) copy-start(f32[128,8,128]{0,2,1:T(8,128)} %copy.171) | copy-start | bytes 1572868
  218.0 25.3 %copy-start.7 = (f32[1,256,8,128]{1,3,2,0:T(8,128)S(1)}, f32[1,256,8,128]{1,3,2,0:T(8,128)}, u32[]{:S(2)}) copy-start(f32[1,256,8,128]{1,3,2,0:T(8,128)} %copy-done.6) | copy-start | bytes 3145732
  218.0 25.3 %copy-start.9 = (f32[1,256,8,128]{1,3,2,0:T(8,128)S(1)}, f32[1,256,8,128]{1,3,2,0:T(8,128)}, u32[]{:S(2)}) copy-start(f32[1,256,8,128]{1,3,2,0:T(8,128)} %copy-done.8) | copy-start | bytes 3145732
  224.9 19.8 %copy-start.23 = (f32[128,8,128]{0,2,1:T(8,128)S(1)}, f32[128,8,128]{0,2,1:T(8,128)}, u32[]{:S(2)}) copy-start(f32[128,8,128]{0,2,1:T(8,128)} %copy.177) | copy-start | bytes 1572868
  (17 other events, 31.2 us)
Sparse Core Ops, SparseCore 0:
  12.9 81.4 all-reduce.10
  124.6 80.9 all-reduce.8
  209.8 87.7 reduce-scatter.4
Sparse Core Ops, SparseCore 1:
  14.5 37.0 all-gather.1
  107.2 70.4 reduce-scatter.2
where the time goes:
time: 306 us; the launch traced here: 305 us
  waiting for transfers between devices  193 us (63%)
  local copies, waits for them, and re-layouts  44.3 us (14%)
  matrix products  25 us (8%)
  between operations  15.7 us (5%)
  other arithmetic  14.2 us (5%)
  starting transfers between devices  12.3 us (4%)
    reduce_scatter x1, waiting for transfers between devices, body(): lax.psum_scatter(partial_sum, 'ctx', scatter_dimension=1, tiled=True)  51.6 us
    psum x1, waiting for transfers between devices, spread(): return lax.psum(block, axis)  49.3 us
    reduce_scatter x1, waiting for transfers between devices, body(): lax.psum_scatter(lax.dot_general(attended_rows, grad_output, (((0,), (0,)...  41.4 us
    ppermute x4, waiting for transfers between devices, shifted(): lax.ppermute(value, axis, [(source, source + steps) for source in range(l...  40.3 us
    dot_general x12, matrix products, product(): return jnp.einsum(form, left, right, preferred_element_type=jnp.float32)  14.7 us
    unnamed x71, local copies, waits for them, and re-layouts  13.7 us
    ppermute x4, starting transfers between devices, shifted(): lax.ppermute(value, axis, [(source, source + steps) for source in range(l...  11.9 us
    psum x1, waiting for transfers between devices, body(): sink_key_sum, sink_value_sum = lax.psum((sink_key, sink_value), 'ctx')  9.86 us
  transfers between devices with their start and end apart: 9, of which 8 were waited for; matrix products, arithmetic and copies ran while one was open for 24% of the time, Pallas kernels for 0%

commit v1 on v0

--- a/solution.py
+++ b/solution.py
@@ -2,6 +2,7 @@
 import jax.numpy as jnp
 from jax import lax
 from jax.sharding import PartitionSpec as P
+from jax.lax import all_gather
 
 HEADS = 8
 HDIM = 128
@@ -19,7 +20,7 @@
 
 def spread(block, axis, holder):
     block = jnp.where(lax.axis_index(axis) == holder, block, jnp.zeros_like(block))
-    return lax.psum(block, axis)
+    return jnp.sum(all_gather(block, axis_name=axis), axis=0)
 
 
 def product(form, left, right):

time: 306 us -> 405 us (1.32)
  waiting for transfers between devices: 193 us -> 292 us
  other arithmetic: 14.2 us -> 22.2 us
  local copies, waits for them, and re-layouts: 44.3 us -> 37.4 us
    psum x1, waiting for transfers between devices: 9.86 us -> 79.1 us  [body(): sink_key_sum, sink_value_sum = lax.psum((sink_key, sink_value), 'ctx')]
    all_gather x0 -> x2, waiting for transfers between devices: none -> 69 us  [spread(): return jnp.sum(all_gather(block, axis_name=axis), axis=0)]
    psum x1 -> x0, waiting for transfers between devices: 49.3 us -> none  [spread(): return lax.psum(block, axis)]
    ppermute x4, waiting for transfers between devices: 40.3 us -> 13.7 us  [shifted(): lax.ppermute(value, axis, [(source, source + steps) for source in range(l...]
    all_gather x1, waiting for transfers between devices: 0.01 us -> 18.2 us  [body(): full_weight = lax.all_gather(proj_weight, 'dp', axis=0, tiled=True)]
    reduce_scatter x1, waiting for transfers between devices: 51.6 us -> 61.3 us  [body(): lax.psum_scatter(partial_sum, 'ctx', scatter_dimension=1, tiled=True)]
    reduce_scatter x1, waiting for transfers between devices: 41.4 us -> 49.6 us  [body(): lax.psum_scatter(lax.dot_general(attended_rows, grad_output, (((0,), (0,)...]
    reduce_sum x0 -> x2, other arithmetic: none -> 4.69 us  [spread(): return jnp.sum(all_gather(block, axis_name=axis), axis=0)]
  transfers between devices with their start and end apart: 9 -> 10, of which waited for: 8 -> 8; matrix products, arithmetic and copies ran while one was open for 24% -> 19% of each run, Pallas kernels for 0% -> 0%
where the time goes in v1:
time: 405 us; the launch traced here: 403 us
  waiting for transfers between devices  292 us (72%)
  local copies, waits for them, and re-layouts  37.4 us (9%)
  matrix products  25 us (6%)
  other arithmetic  22.2 us (5%)
  between operations  14.7 us (4%)
  starting transfers between devices  12.4 us (3%)
    psum x1, waiting for transfers between devices, body(): sink_key_sum, sink_value_sum = lax.psum((sink_key, sink_value), 'ctx')  79.1 us
    all_gather x2, waiting for transfers between devices, spread(): return jnp.sum(all_gather(block, axis_name=axis), axis=0)  69 us
    reduce_scatter x1, waiting for transfers between devices, body(): lax.psum_scatter(partial_sum, 'ctx', scatter_dimension=1, tiled=True)  61.3 us
    reduce_scatter x1, waiting for transfers between devices, body(): lax.psum_scatter(lax.dot_general(attended_rows, grad_output, (((0,), (0,)...  49.6 us
    all_gather x1, waiting for transfers between devices, body(): full_weight = lax.all_gather(proj_weight, 'dp', axis=0, tiled=True)  18.2 us
    dot_general x12, matrix products, product(): return jnp.einsum(form, left, right, preferred_element_type=jnp.float32)  14.8 us
    ppermute x4, waiting for transfers between devices, shifted(): lax.ppermute(value, axis, [(source, source + steps) for source in range(l...  13.7 us
    ppermute x4, starting transfers between devices, shifted(): lax.ppermute(value, axis, [(source, source + steps) for source in range(l...  12 us
  transfers between devices with their start and end apart: 10, of which 8 were waited for; matrix products, arithmetic and copies ran while one was open for 19% of the time, Pallas kernels for 0%

profile of v1, /device:TPU:0, one launch (start us, length us, event | category | flops | bytes accessed | tf_op | source)
XLA Modules:
  0.0 403.5 jit_solution(18224590047643842010)
XLA Ops:
  11.9 5.7 %collective-permute-start = (bf16[256,1024]{0,1:T(8,128)(2,1)S(1)}, bf16[256,1024]{0,1:T(8,128)(2,1)}, u32[]{:S(2)}, u32[]{:S(2)}) collective-permute-start(bf16[256,1024]{0,1:T(8,128)(2,1)S(1)} %bitcast.145), channel_id=1, source_target_pairs={{0,4},{4,8},{8,12},{12,16},{16,20},{20,24},{24,28},{1,5},{5,9},{9,... | collective-permute-start | bytes 1572872 | tf_op jit(solution)/shard_map/ppermute | solution.py:18
  17.8 3.5 collective-permute-start.1
  26.3 5.6 %collective-permute-done = bf16[256,1024]{0,1:T(8,128)(2,1)} collective-permute-done((bf16[256,1024]{0,1:T(8,128)(2,1)S(1)}, bf16[256,1024]{0,1:T(8,128)(2,1)}, u32[]{:S(2)}, u32[]{:S(2)}) %collective-permute-start) | collective-permute-done | bytes 524320 | tf_op jit(solution)/shard_map/ppermute | solution.py:18
  33.9 8.1 %collective-permute-done.1 = bf16[256,1024]{0,1:T(8,128)(2,1)} collective-permute-done((bf16[256,1024]{0,1:T(8,128)(2,1)S(1)}, bf16[256,1024]{0,1:T(8,128)(2,1)}, u32[]{:S(2)}, u32[]{:S(2)}) %collective-permute-start.1) | collective-permute-done | bytes 524320 | tf_op jit(solution)/shard_map/ppermute | solution.py:18
  45.9 23.6 %all-gather.4.cloned.1.call-done = bf16[8,128,1024]{2,1,0:T(8,128)(2,1)} async-done(((bf16[1,128,1024]{2,1,0:T(8,128)(2,1)}), bf16[8,128,1024]{2,1,0:T(8,128)(2,1)}) %all-gather.4.cloned.1.call-update) | async-done | bytes 2097168 | tf_op jit(solution)/shard_map/all_gather | solution.py:23
  72.3 2.3 fusion.47
  74.7 45.4 %all-gather.6.cloned.1.call-done = bf16[8,128,1024]{2,1,0:T(8,128)(2,1)} async-done(((bf16[1,128,1024]{2,1,0:T(8,128)(2,1)}), bf16[8,128,1024]{2,1,0:T(8,128)(2,1)}) %all-gather.6.cloned.1.call-update) | async-done | bytes 2097168 | tf_op jit(solution)/shard_map/all_gather | solution.py:23
  120.1 2.7 reduce_sum.54
  129.4 4.6 %convolution_multiply_fusion = f32[1024,2048]{1,0:T(8,128)} fusion(bf16[1,256,2048]{2,1,0:T(8,128)(2,1)S(1)} %copy-done, bf16[32,8,8,128]{3,2,1,0:T(8,128)(2,1)S(1)} %bitcast.154), kind=kOutput, calls=%fused_computation | convolution fusion | flops 1075838976 | bytes 9961472 | tf_op jit(solution)/shard_map/dot_general | solution.py:160
  134.1 2.4 copy.152
  136.5 18.2 %all-gather.8.cloned.1.call-done = bf16[1024,2048]{1,0:T(8,128)(2,1)} async-done(((bf16[256,2048]{1,0:T(8,128)(2,1)}), bf16[1024,2048]{1,0:T(8,128)(2,1)}) %all-gather.8.cloned.1.call-update) | async-done | bytes 4194320 | tf_op jit(solution)/shard_map/all_gather | solution.py:137
  154.7 3.5 convolution_convert_fusion.1
  161.3 2.1 copy.172
  164.2 2.4 convolution_bitcast_fusion.6
  170.5 2.1 multiply_convert_fusion
  174.8 2.1 copy.162
  176.9 2.1 convert_element_type.83
  178.9 49.6 %reduce-scatter.3.cloned.1.call-done = f32[256,2048]{1,0:T(8,128)} async-done(((f32[1024,2048]{1,0:T(8,128)}), f32[256,2048]{1,0:T(8,128)}) %reduce-scatter.3.cloned.1.call-update) | async-done | bytes 2097168 | tf_op jit(solution)/shard_map/reduce_scatter | solution.py:159
  233.1 2.6 copy.166
  235.6 2.2 pad_add_fusion.1
  242.6 2.2 fusion
  244.9 79.1 %all-reduce.7.cloned.1.call-done = (f32[128,8,128]{2,0,1:T(8,128)}, f32[128,8,128]{2,0,1:T(8,128)}) async-done(((f32[128,8,128]{2,0,1:T(8,128)}, f32[128,8,128]{2,0,1:T(8,128)}), (f32[128,8,128]{2,0,1:T(8,128)}, f32[128,8,128]{2,0,1:T(8,128)})) %all-reduce.7.cloned.1.call-update) | async-done | bytes 1048592 | tf_op jit(solution)/shard_map/psum | solution.py:188
  325.9 2.0 copy.169
  335.3 61.3 %reduce-scatter.5.cloned.1.call-done = f32[256,256]{1,0:T(8,128)} async-done(((f32[256,2048]{1,0:T(8,128)}), f32[256,256]{1,0:T(8,128)}) %reduce-scatter.5.cloned.1.call-update) | async-done | bytes 262160 | tf_op jit(solution)/shard_map/reduce_scatter | solution.py:168
  (149 shorter events, 53.4 us)
Async XLA Ops:
  7.2 122.3 %copy-start = (bf16[1,256,2048]{2,1,0:T(8,128)(2,1)S(1)}, bf16[1,256,2048]{2,1,0:T(8,128)(2,1)}, u32[]{:S(2)}) copy-start(bf16[1,256,2048]{2,1,0:T(8,128)(2,1)} %param.9) | copy-start | bytes 3145732
  7.2 10.4 %copy-start.25 = (bf16[1,256,1024]{2,1,0:T(8,128)(2,1)S(1)}, bf16[1,256,1024]{2,1,0:T(8,128)(2,1)}, u32[]{:S(2)}) copy-start(bf16[1,256,1024]{2,1,0:T(8,128)(2,1)} %param.7) | copy-start | bytes 1572868
  7.2 4.5 %copy-start.24 = (bf16[1,256,1024]{2,1,0:T(8,128)(2,1)S(1)}, bf16[1,256,1024]{2,1,0:T(8,128)(2,1)}, u32[]{:S(2)}) copy-start(bf16[1,256,1024]{2,1,0:T(8,128)(2,1)} %param.8) | copy-start | bytes 1572868
  7.2 62.4 %all-gather.4.cloned.1.call-start = ((), (), s32[]{:S(2)}) async-start(), calls=%async_computation.2 | async-start | bytes 2359296 | tf_op jit(solution)/shard_map/all_gather | solution.py:23
  9.1 111.0 %all-gather.6.cloned.1.call-start = ((), (), s32[]{:S(2)}) async-start(), calls=%async_computation.3 | async-start | bytes 2359296 | tf_op jit(solution)/shard_map/all_gather | solution.py:23
  10.9 143.8 %all-gather.8.cloned.1.call-start = ((), (), s32[]{:S(2)}) async-start(), calls=%async_computation.4 | async-start | bytes 5242880 | tf_op jit(solution)/shard_map/all_gather | solution.py:137
  11.6 216.9 %reduce-scatter.3.cloned.1.call-start = ((), (), s32[]{:S(2)}) async-start(), calls=%async_computation.5 | async-start | bytes 10485760 | tf_op jit(solution)/shard_map/reduce_scatter | solution.py:159
  11.9 20.0 %collective-permute-start = (bf16[256,1024]{0,1:T(8,128)(2,1)S(1)}, bf16[256,1024]{0,1:T(8,128)(2,1)}, u32[]{:S(2)}, u32[]{:S(2)}) collective-permute-start(bf16[256,1024]{0,1:T(8,128)(2,1)S(1)} %bitcast.145), channel_id=1, source_target_pairs={{0,4},{4,8},{8,12},{12,16},{16,20},{20,24},{24,28},{1,5},{5,9},{9,... | collective-permute-start | bytes 1572872 | tf_op jit(solution)/shard_map/ppermute | solution.py:18
  17.8 24.2 %collective-permute-start.1 = (bf16[256,1024]{0,1:T(8,128)(2,1)S(1)}, bf16[256,1024]{0,1:T(8,128)(2,1)}, u32[]{:S(2)}, u32[]{:S(2)}) collective-permute-start(bf16[256,1024]{0,1:T(8,128)(2,1)S(1)} %bitcast.142), channel_id=1, source_target_pairs={{0,4},{4,8},{8,12},{12,16},{16,20},{20,24},{24,28},{1,5},{5,9},{9,... | collective-permute-start | bytes 1572872 | tf_op jit(solution)/shard_map/ppermute | solution.py:18
  21.3 4.3 %copy-start.29 = (s32[1,8,16,2]{2,3,1,0:T(2,128)S(1)}, s32[1,8,16,2]{2,3,1,0:T(2,128)}, u32[]{:S(2)}) copy-start(s32[1,8,16,2]{2,3,1,0:T(2,128)} %param.11) | copy-start | bytes 3076
  23.4 10.4 %copy-start.8 = (bf16[32,8,8,128]{3,2,1,0:T(8,128)(2,1)}, bf16[32,8,8,128]{3,2,1,0:T(8,128)(2,1)S(1)}, u32[]{:S(2)}) copy-start(bf16[32,8,8,128]{3,2,1,0:T(8,128)(2,1)S(1)} %copy.201) | copy-start | bytes 1572868
  134.0 190.0 %all-reduce.7.cloned.1.call-start = ((), (), s32[]{:S(2)}) async-start(), calls=%async_computation.7 | async-start | bytes 2097152 | tf_op jit(solution)/shard_map/psum | solution.py:188
  159.3 4.8 %copy-start.3 = (f32[2,8,128,128]{2,3,0,1:T(8,128)S(1)}, f32[2,8,128,128]{2,3,0,1:T(8,128)}, u32[]{:S(2)}) copy-start(f32[2,8,128,128]{2,3,0,1:T(8,128)} %get-tuple-element.29) | copy-start | bytes 3145732
  163.4 3.1 copy-start.16
  164.2 3.5 copy-start.9
  168.8 227.8 %reduce-scatter.5.cloned.1.call-start = ((), (), s32[]{:S(2)}) async-start(), calls=%async_computation.6 | async-start | bytes 2359296 | tf_op jit(solution)/shard_map/reduce_scatter | solution.py:168
  235.6 3.5 copy-start.7
  237.8 90.1 %collective-permute-start.2 = (f32[256,1024]{0,1:T(8,128)}, f32[256,1024]{0,1:T(8,128)}, u32[]{:S(2)}, u32[]{:S(2)}) collective-permute-start(f32[256,1024]{0,1:T(8,128)} %pad_add_fusion.1), channel_id=1, source_target_pairs={{4,0},{8,4},{12,8},{16,12},{20,16},{24,20},{28,24},{5,1},{9,5},{13... | collective-permute-start | bytes 3145736 | tf_op jit(solution)/shard_map/ppermute | solution.py:18
  239.6 2.9 copy-start.30
  239.7 2.9 copy-start.19
  240.8 91.9 %collective-permute-start.3 = (f32[256,1024]{0,1:T(8,128)}, f32[256,1024]{0,1:T(8,128)}, u32[]{:S(2)}, u32[]{:S(2)}) collective-permute-start(f32[256,1024]{0,1:T(8,128)} %pad_add_fusion), channel_id=1, source_target_pairs={{4,0},{8,4},{12,8},{16,12},{20,16},{24,20},{28,24},{5,1},{9,5},{13... | collective-permute-start | bytes 3145736 | tf_op jit(solution)/shard_map/ppermute | solution.py:18
  244.9 83.1 %copy-start.4 = (f32[1,256,8,128]{1,3,2,0:T(8,128)S(1)}, f32[1,256,8,128]{1,3,2,0:T(8,128)}, u32[]{:S(2)}) copy-start(f32[1,256,8,128]{1,3,2,0:T(8,128)} %copy.166) | copy-start | bytes 3145732
  329.5 3.2 copy-start.6
  332.7 63.9 %copy-start.1 = (bf16[1,256,2048]{2,1,0:T(8,128)(2,1)S(1)}, bf16[1,256,2048]{2,1,0:T(8,128)(2,1)}, u32[]{:S(2)}) copy-start(bf16[1,256,2048]{2,1,0:T(8,128)(2,1)} %param.9) | copy-start | bytes 3145732
  (17 other events, 26.1 us)
Sparse Core Ops, SparseCore 0:
  10.7 58.8 all-gather.3
  71.7 48.3 all-gather.5
  121.6 32.9 all-gather.7
  157.1 71.3 reduce-scatter.2
  231.9 92.0 all-reduce.6
  328.0 68.5 reduce-scatter.4
